TPU v7x, 32 devices: a whole 2x2x4 slice. The times are simulated.
32 devices in a mesh: rep: 2 (over y), hid: 8 (over z, x), wid: 2 (over core).
Axes of the slice: x: 2, y: 2, z: 4, core: 2. Of those that a mesh axis runs over, the one named last changes fastest.
Arguments:
- states: float32 [32, 8192], P(('rep', 'hid'), 'wid'), parts along dimension 0, may hold values from -6 to 6
- norm_gain: float32 [8192], P('wid'), may hold values from 0.25 to 1.75
- gate_weight: bfloat16 [8192, 16384], P('wid', 'hid'), may hold values from -0.0625 to 0.0625
- up_weight: bfloat16 [8192, 16384], P('wid', 'hid'), may hold values from -0.0625 to 0.0625
- down_weight: bfloat16 [16384, 8192], P('hid', 'wid'), may hold values from -0.046875 to 0.046875
Outputs:
- updated: float32 [32, 8192], P(('rep', 'hid'), 'wid'), parts along dimension 0
There are 2 independent parts, one for each index of `rep`. A program takes and returns all parts, laid end to end along the dimension named above; an argument that names none is the same for every part. Nothing has to cross between parts.
All inputs are finite; a program needn't handle non-finite values.
Results may differ from a plain program's by a relative error of at most 0.0029.
Values may be sent and summed in bfloat16 or wider, within the bound.
No kernel may reach another device: no remote copies, remote signals or barrier semaphores. Data moves between devices by JAX's collectives and lax.ppermute only.
A program may use at most 128 MiB of HBM per device.

v0:
```python
import jax
import jax.numpy as jnp
from jax import lax
from jax.sharding import PartitionSpec as P

D = 8192


def both_parts(block, gate_weight, up_weight):
    gate_part = jnp.dot(block, gate_weight, preferred_element_type=jnp.float32)
    up_part = jnp.dot(block, up_weight, preferred_element_type=jnp.float32)
    return jnp.concatenate([gate_part, up_part], axis=1)


def activate(summed, width):
    return (jax.nn.silu(summed[:, :width]) * summed[:, width:]).astype(jnp.bfloat16)


def local(states, norm_gain, gate_weight, up_weight, down_weight):
    local_power = jnp.sum(states * states, axis=1)
    power = lax.psum(local_power, "wid") / D
    normed = (states * norm_gain[None, :] * lax.rsqrt(power + 1e-05)[:, None]).astype(jnp.bfloat16)
    width = gate_weight.shape[1]
    partial_value = both_parts(
        lax.all_gather(normed, "hid", axis=0, tiled=True), gate_weight, up_weight
    )
    summed = lax.psum(partial_value, "wid")
    hidden = activate(summed, width)
    mixed = lax.psum_scatter(
        jnp.dot(hidden, down_weight, preferred_element_type=jnp.float32),
        "hid",
        scatter_dimension=0,
        tiled=True,
    )
    return states + mixed


def solution(mesh):
    return jax.shard_map(
        local,
        mesh=mesh,
        in_specs=(
            P(("rep", "hid"), "wid"),
            P("wid"),
            P("wid", "hid"),
            P("wid", "hid"),
            P("hid", "wid"),
        ),
        out_specs=P(("rep", "hid"), "wid"),
        check_vma=False,
    )
```

profile of v0, /device:TPU:0, one launch (start us, length us, event | category | flops | bytes accessed | tf_op | source)
XLA Modules:
  0.0 165.8 jit_solution(5688162967370934781)
XLA Ops:
  6.5 0.0 all-reduce.4.cloned.1.call-start
  6.5 0.9 multiply_reduce_fusion
  7.4 2.6 %psum.14 = f32[2]{0:T(128)S(1)} all-reduce(f32[2]{0:T(128)S(1)} %multiply_reduce_fusion), channel_id=1, replica_groups=mesh['rep'=2,'hid'=8,'wid'=2] {'wid'}, use_global_device_ids=true, to_apply=%region_1.0 | all-reduce | flops 2 | bytes 16 | tf_op jit(solution)/shard_map/psum | solution.py:21
  10.1 0.8 fusion.4
  10.9 32.2 %all-gather = bf16[8,2,4096]{2,1,0:T(2,128)(2,1)S(1)} all-gather(bf16[1,2,4096]{2,1,0:T(2,128)(2,1)S(1)} %fusion.4), channel_id=1, replica_groups=mesh['rep'=2,'hid'=8,'wid'=2] {'hid'}, dimensions={0}, use_global_device_ids=true | all-gather | bytes 147456 | tf_op jit(solution)/shard_map/all_gather | solution.py:25
  43.1 0.1 reshape.3
  43.2 0.0 copy-start
  43.2 8.2 %fusion.6 = f32[16,2048]{1,0:T(8,128)S(1)} fusion(bf16[16,4096]{1,0:T(8,128)(2,1)S(1)} %reshape.3, bf16[4096,2048]{1,0:T(8,128)(2,1)} %param.7), kind=kOutput, calls=%fused_computation.11 | convolution fusion | flops 268435456 | bytes 17039360 | tf_op jit(solution)/shard_map/dot_general | solution.py:10
  51.4 2.3 %copy-done = bf16[4096,2048]{1,0:T(8,128)(2,1)S(1)} copy-done((bf16[4096,2048]{1,0:T(8,128)(2,1)S(1)}, bf16[4096,2048]{1,0:T(8,128)(2,1)}, u32[]{:S(2)}) %copy-start) | copy-done | bytes 16777240
  53.7 2.3 %fusion.7 = f32[16,2048]{1,0:T(8,128)S(1)} fusion(bf16[16,4096]{1,0:T(8,128)(2,1)S(1)} %reshape.3, bf16[4096,2048]{1,0:T(8,128)(2,1)S(1)} %copy-done), kind=kOutput, calls=%fused_computation.12 | convolution fusion | flops 268435456 | bytes 17039360 | tf_op jit(solution)/shard_map/dot_general | solution.py:11
  56.0 0.0 copy-start.2
  56.0 0.0 copy-start.1
  56.0 0.7 pad_maximum_fusion
  56.7 0.0 all-reduce.4.cloned.1.call-update
  56.7 0.0 all-reduce.6.cloned.1.call-start
  56.8 19.3 %all-reduce.4.cloned.1.call-done = f32[16,4096]{1,0:T(8,128)} async-done(((f32[16,4096]{1,0:T(8,128)}), f32[16,4096]{1,0:T(8,128)}) %all-reduce.4.cloned.1.call-update) | async-done | bytes 262160 | tf_op jit(solution)/shard_map/psum | solution.py:27
  76.1 8.9 %fusion.1 = f32[16,4096]{1,0:T(8,128)} fusion(bf16[2048,4096]{1,0:T(8,128)(2,1)} %param.9, f32[16,4096]{1,0:T(8,128)} %all-reduce.4.cloned.1.call-done), kind=kOutput, calls=%fused_computation.3 | convolution fusion | flops 268632064 | bytes 17301504 | tf_op jit(solution)/shard_map/dot_general | solution.py:30
  85.0 0.0 all-reduce.6.cloned.1.call-update
  85.0 0.0 copy-done.2
  85.1 0.6 dynamic-slice
  86.3 71.1 %all-reduce.6.cloned.1.call-done = f32[16,4096]{1,0:T(8,128)} async-done(((f32[16,4096]{1,0:T(8,128)}), f32[16,4096]{1,0:T(8,128)}) %all-reduce.6.cloned.1.call-update) | async-done | bytes 262160
  157.4 0.0 copy-done.1
  157.4 1.5 dynamic-slice_add_fusion
  (1 shorter events, 0.0 us)
Async XLA Ops:
  6.5 69.6 %all-reduce.4.cloned.1.call-start = ((), (), s32[]{:S(2)}) async-start(), calls=%async_computation | async-start | bytes 524288 | tf_op jit(solution)/shard_map/psum | solution.py:27
  43.2 10.5 %copy-start = (bf16[4096,2048]{1,0:T(8,128)(2,1)S(1)}, bf16[4096,2048]{1,0:T(8,128)(2,1)}, u32[]{:S(2)}) copy-start(bf16[4096,2048]{1,0:T(8,128)(2,1)} %param.8) | copy-start | bytes 50331652
  56.0 29.1 %copy-start.2 = (u32[32]{0:T(128)S(1)}, u32[32]{0:T(128)}, u32[]{:S(2)}) copy-start(u32[32]{0:T(128)} %constant.13) | copy-start | bytes 388
  56.0 101.4 %copy-start.1 = (f32[2,4096]{1,0:T(2,128)S(1)}, f32[2,4096]{1,0:T(2,128)}, u32[]{:S(2)}) copy-start(f32[2,4096]{1,0:T(2,128)} %param.5) | copy-start | bytes 98308
  56.7 100.7 %all-reduce.6.cloned.1.call-start = ((), (), s32[]{:S(2)}) async-start(), calls=%async_computation.1 | async-start | bytes 524288
Sparse Core Ops, SparseCore 0:
  56.9 19.2 all-reduce.3
  85.2 72.2 all-reduce.5
where the time goes:
time: 166 us
  waiting for transfers between devices  90.5 us (55%)
  blocking collectives  34.8 us (21%)
  matrix products  19.4 us (12%)
  between operations  14.1 us (8%)
  other arithmetic  4.02 us (2%)
  local copies, waits for them, and re-layouts  2.98 us (2%)
    unnamed x3, waiting for transfers between devices  71.2 us
    all_gather x1, blocking collectives, local(): lax.all_gather(normed, 'hid', axis=0, tiled=True)  32.2 us
    psum x1, waiting for transfers between devices, local(): summed = lax.psum(partial_value, 'wid')  19.3 us
    dot_general x1, matrix products, local(): jnp.dot(hidden, down_weight, preferred_element_type=jnp.float32)  8.91 us
    dot_general x1, matrix products, both_parts(): gate_part = jnp.dot(block, gate_weight, preferred_element_type=jnp.float32)  8.2 us
  transfers between devices with their start and end apart: 2, of which 2 were waited for; matrix products, arithmetic and copies ran while one was open for 0% of the time, Pallas kernels for 0%

commit v1 on v0

v1 whole, which is shorter than its diff:
```python
import jax
import jax.numpy as jnp
from jax import lax
from jax.experimental import pallas as pl
from jax.experimental.pallas import tpu as pltpu
from jax.sharding import PartitionSpec as P

EPS = 1e-05
F32, BF16 = jnp.float32, jnp.bfloat16


def call(kernel, out, *args, name, flops=0, scratch=(), limit=4 << 20):
    spec = pl.BlockSpec(memory_space=pltpu.VMEM)
    return pl.pallas_call(
        kernel,
        out_shape=out,
        in_specs=[spec] * len(args),
        out_specs=spec,
        scratch_shapes=scratch,
        compiler_params=pltpu.CompilerParams(vmem_limit_bytes=limit),
        cost_estimate=pl.CostEstimate(flops=flops, bytes_accessed=0, transcendentals=0),
        name=name,
    )(*args)


def dot(a, b):
    return jnp.dot(a, b, preferred_element_type=F32)


def prepare_kernel(states_ref, others_ref, gain_ref, out_ref):
    states, others = states_ref[...], others_ref[...]
    squares = jnp.sum(states * states, axis=1, keepdims=True)
    squares += jnp.sum(others * others, axis=1, keepdims=True)
    scale = lax.rsqrt(squares / (2 * states.shape[1]) + EPS)
    normed = (states * gain_ref[...] * scale).astype(BF16)
    for k in range(out_ref.shape[0]):
        out_ref[k] = normed


def project_kernel(gathered_ref, weight_ref, out_ref):
    x = gathered_ref[...].reshape(out_ref.shape[0], weight_ref.shape[0])
    out_ref[...] = dot(x, weight_ref[...])


def down_kernel(gate_ref, gate_other_ref, up_ref, up_other_ref, down_ref, out_ref):
    gate = gate_ref[...] + gate_other_ref[...]
    up = up_ref[...] + up_other_ref[...]
    hidden = (gate / (1 + jnp.exp(-gate)) * up).astype(BF16)
    out_ref[...] = dot(hidden, down_ref[...]).astype(BF16).reshape(out_ref.shape)


def finish_kernel(states_ref, parts_ref, out_ref):
    total = states_ref[...]
    for k in range(parts_ref.shape[0]):
        total += parts_ref[k].astype(F32)
    out_ref[...] = total


def solution(mesh):
    hid = mesh.shape["hid"]

    def local(states, norm_gain, gate_weight, up_weight, down_weight):
        rows, half = states.shape
        width = gate_weight.shape[1]
        streams = rows * hid
        struct = jax.ShapeDtypeStruct

        def swap(value):
            return lax.ppermute(value, "wid", [(0, 1), (1, 0)])

        normed = call(
            prepare_kernel,
            struct((hid, rows, half), BF16),
            states,
            swap(states),
            norm_gain[None, :],
            name="prepare",
            flops=100_000_000_000,
            limit=1 << 20,
        )
        gathered = lax.all_to_all(normed, "hid", 0, 0)
        part = struct((streams, width), F32)
        gate = call(project_kernel, part, gathered, gate_weight, name="gate")
        up = call(project_kernel, part, gathered, up_weight, name="up")
        mixed = call(
            down_kernel,
            struct((hid, rows, half), BF16),
            gate,
            swap(gate),
            up,
            swap(up),
            down_weight,
            name="down",
        )
        parts = lax.all_to_all(mixed, "hid", 0, 0)
        return call(finish_kernel, struct((rows, half), F32), states, parts, name="finish")

    return jax.shard_map(
        local,
        mesh=mesh,
        in_specs=(
            P(("rep", "hid"), "wid"),
            P("wid"),
            P("wid", "hid"),
            P("wid", "hid"),
            P("hid", "wid"),
        ),
        out_specs=P(("rep", "hid"), "wid"),
        check_vma=False,
    )
```

time: 166 us -> 37.2 us (0.22)
  waiting for transfers between devices: 90.5 us -> 2.06 us
  matrix products: 19.4 us -> 0 us
  between operations: 14.1 us -> 0.04 us
  blocking collectives: 34.8 us -> 24.7 us
  Pallas kernels: 0 us -> 7.6 us
  other arithmetic: 4.02 us -> 0 us
    unnamed x3 -> x0, waiting for transfers between devices: 71.2 us -> none
    all_gather x1 -> x0, blocking collectives: 32.2 us -> none  [local(): lax.all_gather(normed, 'hid', axis=0, tiled=True)]
    all_to_all x0 -> x2, blocking collectives: none -> 24.7 us  [the longest x1 14.5 us: local(): gathered = lax.all_to_all(normed, 'hid', 0, 0)]
    dot_general x3 -> x0, matrix products: 19.4 us -> none  [the longest x1 8.91 us: local(): jnp.dot(hidden, down_weight, preferred_element_type=jnp.float32)]
    psum x1 -> x0, waiting for transfers between devices: 19.3 us -> none  [local(): summed = lax.psum(partial_value, 'wid')]
    pallas_call x0 -> x5, Pallas kernels: none -> 7.6 us  [call(): pl.pallas_call(kernel, out_shape=out, in_specs=[spec] * len(args), out_sp...]
    psum x1 -> x0, blocking collectives: 2.62 us -> none  [local(): power = lax.psum(local_power, 'wid') / D]
    ppermute x0 -> x3, waiting for transfers between devices: none -> 2.06 us  [swap(): return lax.ppermute(value, 'wid', [(0, 1), (1, 0)])]
  transfers between devices with their start and end apart: 2 -> 3, of which waited for: 2 -> 2; matrix products, arithmetic and copies ran while one was open for 0% -> 0% of each run, Pallas kernels for 0% -> 6%
where the time goes in v1:
time: 37.2 us; the launch traced here: 36.9 us
  blocking collectives  24.7 us (66%)
  Pallas kernels  7.6 us (20%)
  waiting for transfers between devices  2.06 us (6%)
  local copies, waits for them, and re-layouts  1.5 us (4%)
  starting transfers between devices  1.01 us (3%)
    all_to_all x1, blocking collectives, local(): gathered = lax.all_to_all(normed, 'hid', 0, 0)  14.5 us
    all_to_all x1, blocking collectives, local(): parts = lax.all_to_all(mixed, 'hid', 0, 0)  10.2 us
    pallas_call x5, Pallas kernels, call(): pl.pallas_call(kernel, out_shape=out, in_specs=[spec] * len(args), out_sp...  7.6 us
    ppermute x3, waiting for transfers between devices, swap(): return lax.ppermute(value, 'wid', [(0, 1), (1, 0)])  2.06 us
    unnamed x12, local copies, waits for them, and re-layouts  1.5 us
    ppermute x3, starting transfers between devices, swap(): return lax.ppermute(value, 'wid', [(0, 1), (1, 0)])  1.01 us
  transfers between devices with their start and end apart: 3, of which 2 were waited for; matrix products, arithmetic and copies ran while one was open for 0% of the time, Pallas kernels for 6%

profile of v1, /device:TPU:0, one launch (start us, length us, event | category | flops | bytes accessed | tf_op | source)
XLA Modules:
  0.0 36.9 jit_solution(11418478085109424558)
XLA Ops:
  0.0 0.5 %collective-permute-start = (f32[2,4096]{1,0:T(2,128)}, f32[2,4096]{1,0:T(2,128)S(1)}, u32[]{:S(2)}, u32[]{:S(2)}) collective-permute-start(f32[2,4096]{1,0:T(2,128)} %states_ref.3), channel_id=1, source_target_pairs={{0,1},{1,0},{2,3},{3,2},{4,5},{5,4},{6,7},{7,6},{8,9},{9,8},{10,11... | collective-permute-start | bytes 98312 | tf_op jit(solution)/shard_map/ppermute | solution.py:69
  0.5 1.1 %collective-permute-done.others_ref = f32[2,4096]{1,0:T(2,128)S(1)} collective-permute-done((f32[2,4096]{1,0:T(2,128)}, f32[2,4096]{1,0:T(2,128)S(1)}, u32[]{:S(2)}, u32[]{:S(2)}) %collective-permute-start) | collective-permute-done | bytes 32800 | tf_op jit(solution)/shard_map/ppermute | solution.py:69
  1.6 0.0 copy-start.3
  1.6 0.8 %copy-done.3 = f32[2,4096]{1,0:T(2,128)S(1)} copy-done((f32[2,4096]{1,0:T(2,128)S(1)}, f32[2,4096]{1,0:T(2,128)}, u32[]{:S(2)}) %copy-start.3) | copy-done | bytes 32792
  2.3 0.0 copy-start.5
  2.3 0.7 %copy-done.5 = f32[4096]{0:T(1024)S(1)} copy-done((f32[4096]{0:T(1024)S(1)}, f32[4096]{0:T(1024)}, u32[]{:S(2)}) %copy-start.5) | copy-done | bytes 16408
  3.0 0.0 copy-start
  3.0 0.1 prepare.1
  3.2 0.0 copy-start.1
  3.2 14.5 %all_to_all.10.gathered_ref = bf16[8,2,4096]{2,1,0:T(2,128)(2,1)S(1)} all-to-all(bf16[8,2,4096]{2,1,0:T(2,128)(2,1)S(1)} %prepare.1), channel_id=1, replica_groups=mesh['rep'=2,'hid'=8,'wid'=2] {'hid'}, dimensions={0} | all-to-all | bytes 262144 | tf_op jit(solution)/shard_map/all_to_all | solution.py:81
  17.7 0.0 copy-done
  17.8 0.0 copy-start.2
  17.8 2.3 %gate.1.gate_ref = f32[16,2048]{1,0:T(8,128)S(1)} custom-call(bf16[8,2,4096]{2,1,0:T(2,128)(2,1)S(1)} %all_to_all.10.gathered_ref, bf16[4096,2048]{1,0:T(8,128)(2,1)S(1)} %copy-done), custom_call_target="tpu_custom_call" | custom-call | tf_op jit(solution)/shard_map/gate/pallas_call | solution.py:14
  20.0 0.0 copy-start.4
  20.0 0.0 collective-permute-start.1
  20.0 0.0 copy-done.1
  20.0 2.3 %up.1.up_ref = f32[16,2048]{1,0:T(8,128)S(1)} custom-call(bf16[8,2,4096]{2,1,0:T(2,128)(2,1)S(1)} %all_to_all.10.gathered_ref, bf16[4096,2048]{1,0:T(8,128)(2,1)S(1)} %copy-done.1), custom_call_target="tpu_custom_call" | custom-call | tf_op jit(solution)/shard_map/up/pallas_call | solution.py:14
  22.3 0.5 %collective-permute-start.2 = (f32[16,2048]{1,0:T(8,128)S(1)}, f32[16,2048]{1,0:T(8,128)S(1)}, u32[]{:S(2)}, u32[]{:S(2)}) collective-permute-start(f32[16,2048]{1,0:T(8,128)S(1)} %up.1.up_ref), channel_id=1, source_target_pairs={{0,1},{1,0},{2,3},{3,2},{4,5},{5,4},{6,7},{7,6},{8,9},{9,8},{10,11... | collective-permute-start | bytes 393224 | tf_op jit(solution)/shard_map/ppermute | solution.py:69
  22.8 0.0 collective-permute-done.1.gate_other_ref
  22.8 1.0 %collective-permute-done.2.up_other_ref = f32[16,2048]{1,0:T(8,128)S(1)} collective-permute-done((f32[16,2048]{1,0:T(8,128)S(1)}, f32[16,2048]{1,0:T(8,128)S(1)}, u32[]{:S(2)}, u32[]{:S(2)}) %collective-permute-start.2) | collective-permute-done | bytes 131104 | tf_op jit(solution)/shard_map/ppermute | solution.py:69
  23.8 0.0 copy-done.2
  23.8 2.3 %down.1 = bf16[8,2,4096]{2,1,0:T(2,128)(2,1)S(1)} custom-call(f32[16,2048]{1,0:T(8,128)S(1)} %gate.1.gate_ref, f32[16,2048]{1,0:T(8,128)S(1)} %collective-permute-done.1.gate_other_ref, f32[16,2048]{1,0:T(8,128)S(1)} %up.1.up_ref, f32[16,2048]{1,0:T(8,128)S(1)} %collective-permute-done.2.up_other_ref, bf16[2048,4096]{1,0:T(8,128)(2,1)S(1)} %copy-done.2), custom_call_target="tpu_custom_call" | custom-call | tf_op jit(solution)/shard_map/down/pallas_call | solution.py:14
  26.1 10.2 %all_to_all.11.parts_ref = bf16[8,2,4096]{2,1,0:T(2,128)(2,1)S(1)} all-to-all(bf16[8,2,4096]{2,1,0:T(2,128)(2,1)S(1)} %down.1), channel_id=1, replica_groups=mesh['rep'=2,'hid'=8,'wid'=2] {'hid'}, dimensions={0} | all-to-all | bytes 262144 | tf_op jit(solution)/shard_map/all_to_all | solution.py:95
  36.3 0.0 copy-done.4
  36.3 0.6 %finish.1 = f32[2,4096]{1,0:T(2,128)} custom-call(f32[2,4096]{1,0:T(2,128)S(1)} %copy-done.4, bf16[8,2,4096]{2,1,0:T(2,128)(2,1)S(1)} %all_to_all.11.parts_ref), custom_call_target="tpu_custom_call" | custom-call | tf_op jit(solution)/shard_map/finish/pallas_call | solution.py:14
Async XLA Ops:
  0.0 1.6 %collective-permute-start = (f32[2,4096]{1,0:T(2,128)}, f32[2,4096]{1,0:T(2,128)S(1)}, u32[]{:S(2)}, u32[]{:S(2)}) collective-permute-start(f32[2,4096]{1,0:T(2,128)} %states_ref.3), channel_id=1, source_target_pairs={{0,1},{1,0},{2,3},{3,2},{4,5},{5,4},{6,7},{7,6},{8,9},{9,8},{10,11... | collective-permute-start | bytes 98312 | tf_op jit(solution)/shard_map/ppermute | solution.py:69
  1.6 0.8 %copy-start.3 = (f32[2,4096]{1,0:T(2,128)S(1)}, f32[2,4096]{1,0:T(2,128)}, u32[]{:S(2)}) copy-start(f32[2,4096]{1,0:T(2,128)} %states_ref.3) | copy-start | bytes 98308
  2.3 0.7 %copy-start.5 = (f32[4096]{0:T(1024)S(1)}, f32[4096]{0:T(1024)}, u32[]{:S(2)}) copy-start(f32[4096]{0:T(1024)} %param.6) | copy-start | bytes 49156
  3.0 14.7 %copy-start = (bf16[4096,2048]{1,0:T(8,128)(2,1)S(1)}, bf16[4096,2048]{1,0:T(8,128)(2,1)}, u32[]{:S(2)}) copy-start(bf16[4096,2048]{1,0:T(8,128)(2,1)} %weight_ref.2) | copy-start | bytes 50331652
  3.2 16.8 %copy-start.1 = (bf16[4096,2048]{1,0:T(8,128)(2,1)S(1)}, bf16[4096,2048]{1,0:T(8,128)(2,1)}, u32[]{:S(2)}) copy-start(bf16[4096,2048]{1,0:T(8,128)(2,1)} %weight_ref.3) | copy-start | bytes 50331652
  17.8 6.1 %copy-start.2 = (bf16[2048,4096]{1,0:T(8,128)(2,1)S(1)}, bf16[2048,4096]{1,0:T(8,128)(2,1)}, u32[]{:S(2)}) copy-start(bf16[2048,4096]{1,0:T(8,128)(2,1)} %down_ref.1) | copy-start | bytes 50331652
  20.0 16.3 %copy-start.4 = (f32[2,4096]{1,0:T(2,128)S(1)}, f32[2,4096]{1,0:T(2,128)}, u32[]{:S(2)}) copy-start(f32[2,4096]{1,0:T(2,128)} %states_ref.3) | copy-start | bytes 98308
  20.0 2.8 %collective-permute-start.1 = (f32[16,2048]{1,0:T(8,128)S(1)}, f32[16,2048]{1,0:T(8,128)S(1)}, u32[]{:S(2)}, u32[]{:S(2)}) collective-permute-start(f32[16,2048]{1,0:T(8,128)S(1)} %gate.1.gate_ref), channel_id=1, source_target_pairs={{0,1},{1,0},{2,3},{3,2},{4,5},{5,4},{6,7},{7,6},{8,9},{9,8},{10,11... | collective-permute-start | bytes 393224 | tf_op jit(solution)/shard_map/ppermute | solution.py:69
  22.3 1.5 %collective-permute-start.2 = (f32[16,2048]{1,0:T(8,128)S(1)}, f32[16,2048]{1,0:T(8,128)S(1)}, u32[]{:S(2)}, u32[]{:S(2)}) collective-permute-start(f32[16,2048]{1,0:T(8,128)S(1)} %up.1.up_ref), channel_id=1, source_target_pairs={{0,1},{1,0},{2,3},{3,2},{4,5},{5,4},{6,7},{7,6},{8,9},{9,8},{10,11... | collective-permute-start | bytes 393224 | tf_op jit(solution)/shard_map/ppermute | solution.py:69

commit v2 on v1

v2 whole, which is shorter than its diff:
```python
import jax
import jax.numpy as jnp
from jax import lax
from jax.experimental import pallas as pl
from jax.experimental.pallas import tpu as pltpu
from jax.sharding import PartitionSpec as P

EPS = 1e-05
F32, BF16 = jnp.float32, jnp.bfloat16
VMEM, HBM = pltpu.MemorySpace.VMEM, pltpu.MemorySpace.HBM


def call(kernel, out, *args, name, flops=0, space=VMEM, scratch=(), limit=4 << 20):
    return pl.pallas_call(
        kernel,
        out_shape=out,
        in_specs=[pl.BlockSpec(memory_space=space)] * len(args),
        out_specs=jax.tree.map(lambda _: pl.BlockSpec(memory_space=VMEM), out),
        scratch_shapes=scratch,
        compiler_params=pltpu.CompilerParams(vmem_limit_bytes=limit),
        cost_estimate=pl.CostEstimate(flops=flops, bytes_accessed=0, transcendentals=0),
        name=name,
    )(*args)


def dot(a, b):
    return jnp.dot(a, b, preferred_element_type=F32)


def load_kernel(states_hbm, gain_hbm, scaled_ref, squares_ref, states_ref, gain_ref, sems):
    copies = [
        pltpu.make_async_copy(states_hbm, states_ref, sems.at[0]),
        pltpu.make_async_copy(gain_hbm, gain_ref, sems.at[1]),
    ]
    for copy in copies:
        copy.start()
    for copy in copies:
        copy.wait()
    states = states_ref[...]
    scaled_ref[...] = states * gain_ref[...]
    squares_ref[...] = jnp.sum(states * states, axis=1, keepdims=True)


def prepare_kernel(scaled_ref, squares_ref, others_ref, out_ref):
    others = others_ref[...]
    squares = squares_ref[...] + jnp.sum(others * others, axis=1, keepdims=True)
    scale = lax.rsqrt(squares / (2 * others.shape[1]) + EPS)
    normed = (scaled_ref[...] * scale).astype(BF16)
    for k in range(out_ref.shape[0]):
        out_ref[k] = normed


def first_kernel(gathered_ref, gate_ref, up_ref, out_ref):
    streams, total = out_ref.shape
    width = gate_ref.shape[1]
    x = gathered_ref[...].reshape(streams, gate_ref.shape[0])
    out_ref[:, :width] = dot(x, gate_ref[...])
    out_ref[:, width:] = dot(x, up_ref[:, : total - width])


def second_kernel(gathered_ref, up_ref, *refs):
    out_ref = refs[-1]
    streams, count = out_ref.shape
    x = gathered_ref[...].reshape(streams, up_ref.shape[0])
    out_ref[...] = dot(x, up_ref[:, up_ref.shape[1] - count :])


def activate(gate, up):
    return (gate / (1 + jnp.exp(-gate)) * up).astype(BF16)


def down_kernel(first_ref, first_other_ref, down_ref, out_ref):
    width = down_ref.shape[0]
    count = first_ref.shape[1] - width
    gate = first_ref[:, :count] + first_other_ref[:, :count]
    up = first_ref[:, width:] + first_other_ref[:, width:]
    out = dot(activate(gate, up), down_ref[:count, :])
    out_ref[...] = out.astype(out_ref.dtype).reshape(out_ref.shape)


def add_kernel(first_ref, first_other_ref, second_ref, second_other_ref, down_ref, sum_ref, out_ref):
    width = down_ref.shape[0]
    count = first_ref.shape[1] - width
    gate = first_ref[:, count:width] + first_other_ref[:, count:width]
    up = second_ref[...] + second_other_ref[...]
    out = sum_ref[...] + dot(activate(gate, up), down_ref[count:, :])
    out_ref[...] = out.astype(out_ref.dtype).reshape(out_ref.shape)


def finish_kernel(states_ref, parts_ref, out_ref):
    total = states_ref[...]
    for k in range(parts_ref.shape[0]):
        total += parts_ref[k].astype(F32)
    out_ref[...] = total


def solution(mesh):
    hid = mesh.shape["hid"]

    def local(states, norm_gain, gate_weight, up_weight, down_weight):
        rows, half = states.shape
        width = gate_weight.shape[1]
        streams = rows * hid
        count = width // 2 if width % 256 == 0 else width
        struct = jax.ShapeDtypeStruct

        def swap(value):
            return lax.ppermute(value, "wid", [(0, 1), (1, 0)])

        scaled, squares = call(
            load_kernel,
            (struct((rows, half), F32), struct((rows, 1), F32)),
            pltpu.with_memory_space_constraint(states, HBM),
            pltpu.with_memory_space_constraint(norm_gain[None, :], HBM),
            name="load",
            flops=100_000_000_000,
            space=pl.ANY,
            limit=1 << 20,
            scratch=[
                pltpu.VMEM((rows, half), F32),
                pltpu.VMEM((1, half), F32),
                pltpu.SemaphoreType.DMA((2,)),
            ],
        )
        normed = call(
            prepare_kernel,
            struct((hid, rows, half), BF16),
            scaled,
            squares,
            swap(states),
            name="prepare",
            limit=1 << 20,
        )
        gathered = lax.all_to_all(normed, "hid", 0, 0)

        first = call(
            first_kernel,
            struct((streams, width + count), F32),
            gathered,
            gate_weight,
            up_weight,
            name="first",
            limit=17 << 18,
        )
        first_other = swap(first)
        out = struct((hid, rows, half), BF16)
        if count == width:
            mixed = call(down_kernel, out, first, first_other, down_weight, name="down")
        else:
            second = call(
                second_kernel,
                struct((streams, width - count), F32),
                gathered,
                up_weight,
                name="second",
                limit=4 << 20,
            )
            second_other = swap(second)
            mixed = call(
                down_kernel,
                struct((streams, half), F32),
                first,
                first_other,
                down_weight,
                name="down",
                limit=3 << 20,
            )
            mixed = call(
                add_kernel,
                out,
                first,
                first_other,
                second,
                second_other,
                down_weight,
                mixed,
                name="add",
                limit=3 << 20,
            )
        summands = lax.all_to_all(mixed, "hid", 0, 0)
        return call(finish_kernel, struct((rows, half), F32), states, summands, name="finish")

    return jax.shard_map(
        local,
        mesh=mesh,
        in_specs=(
            P(("rep", "hid"), "wid"),
            P("wid"),
            P("wid", "hid"),
            P("wid", "hid"),
            P("hid", "wid"),
        ),
        out_specs=P(("rep", "hid"), "wid"),
        check_vma=False,
    )
```

time: 37.2 us -> 35.6 us (0.957)
  waiting for transfers between devices: 2.06 us -> 0.02 us
  Pallas kernels: 7.6 us -> 8.85 us
  local copies, waits for them, and re-layouts: 1.5 us -> 0.99 us
    ppermute x3, waiting for transfers between devices: 2.06 us -> 0.02 us  [swap(): return lax.ppermute(value, 'wid', [(0, 1), (1, 0)])]
    pallas_call x5 -> x7, Pallas kernels: 7.6 us -> 8.85 us  [call(): pl.pallas_call(kernel, out_shape=out, in_specs=[pl.BlockSpec(memory_space...]
    unnamed x12 -> x14, local copies, waits for them, and re-layouts: 1.5 us -> 0.99 us
  transfers between devices with their start and end apart: 3 -> 3, of which waited for: 2 -> 0; matrix products, arithmetic and copies ran while one was open for 0% -> 0% of each run, Pallas kernels for 6% -> 10%
where the time goes in v2:
time: 35.6 us; the launch traced here: 35.3 us
  blocking collectives  24.4 us (69%)
  Pallas kernels  8.85 us (25%)
  starting transfers between devices  1.01 us (3%)
  local copies, waits for them, and re-layouts  0.99 us (3%)
    all_to_all x1, blocking collectives, local(): gathered = lax.all_to_all(normed, 'hid', 0, 0)  14.5 us
    all_to_all x1, blocking collectives, local(): summands = lax.all_to_all(mixed, 'hid', 0, 0)  9.82 us
    pallas_call x7, Pallas kernels, call(): pl.pallas_call(kernel, out_shape=out, in_specs=[pl.BlockSpec(memory_space...  8.85 us
    ppermute x3, starting transfers between devices, swap(): return lax.ppermute(value, 'wid', [(0, 1), (1, 0)])  1.01 us
    unnamed x14, local copies, waits for them, and re-layouts  0.99 us
  transfers between devices with their start and end apart: 3, of which 0 were waited for; matrix products, arithmetic and copies ran while one was open for 0% of the time, Pallas kernels for 10%

profile of v2, /device:TPU:0, one launch (start us, length us, event | category | flops | bytes accessed | tf_op | source)
XLA Modules:
  0.0 35.3 jit_solution(876969835331168870)
XLA Ops:
  0.0 0.5 %collective-permute-start = (f32[2,4096]{1,0:T(2,128)}, f32[2,4096]{1,0:T(2,128)S(1)}, u32[]{:S(2)}, u32[]{:S(2)}) collective-permute-start(f32[2,4096]{1,0:T(2,128)} %states_ref.1), channel_id=1, source_target_pairs={{0,1},{1,0},{2,3},{3,2},{4,5},{5,4},{6,7},{7,6},{8,9},{9,8},{10,11... | collective-permute-start | bytes 98312 | tf_op jit(solution)/shard_map/ppermute | solution.py:108
  0.5 0.0 copy-start
  0.5 0.0 copy-start.1
  0.5 1.0 %load.1 = (f32[2,4096]{1,0:T(2,128)S(1)}, f32[2,1]{1,0:T(2,128)S(1)}) custom-call(f32[2,4096]{1,0:T(2,128)} %states_ref.1, f32[1,4096]{1,0:T(1,128)} %bitcast.3), custom_call_target="tpu_custom_call" | custom-call | flops 99999997952 | tf_op jit(solution)/shard_map/load/pallas_call | solution.py:14
  1.5 0.0 collective-permute-done.others_ref
  1.6 0.2 prepare.1
  1.8 14.5 %all_to_all.10.gathered_ref = bf16[8,2,4096]{2,1,0:T(2,128)(2,1)S(1)} all-to-all(bf16[8,2,4096]{2,1,0:T(2,128)(2,1)S(1)} %prepare.1), channel_id=1, replica_groups=mesh['rep'=2,'hid'=8,'wid'=2] {'hid'}, dimensions={0} | all-to-all | bytes 262144 | tf_op jit(solution)/shard_map/all_to_all | solution.py:134
  16.3 0.0 copy-done
  16.3 0.0 copy-done.1
  16.3 0.0 slice-start
  16.3 0.0 slice-start.1
  16.3 0.0 slice-start.2
  16.3 3.3 %first.1.first_ref = f32[16,3072]{1,0:T(8,128)S(1)} custom-call(bf16[8,2,4096]{2,1,0:T(2,128)(2,1)S(1)} %all_to_all.10.gathered_ref, bf16[4096,2048]{1,0:T(8,128)(2,1)S(1)} %copy-done.1, bf16[4096,2048]{1,0:T(8,128)(2,1)S(1)} %copy-done), custom_call_target="tpu_custom_call" | custom-call | tf_op jit(solution)/shard_map/first/pallas_call | solution.py:14
  19.7 0.0 slice-start.3
  19.7 0.0 collective-permute-start.1
  19.7 1.2 %second.1.second_ref = f32[16,1024]{1,0:T(8,128)S(1)} custom-call(bf16[8,2,4096]{2,1,0:T(2,128)(2,1)S(1)} %all_to_all.10.gathered_ref, bf16[4096,2048]{1,0:T(8,128)(2,1)S(1)} %copy-done), custom_call_target="tpu_custom_call" | custom-call | tf_op jit(solution)/shard_map/second/pallas_call | solution.py:14
  20.9 0.0 copy-start.2
  20.9 0.5 %collective-permute-start.2 = (f32[16,1024]{1,0:T(8,128)S(1)}, f32[16,1024]{1,0:T(8,128)S(1)}, u32[]{:S(2)}, u32[]{:S(2)}) collective-permute-start(f32[16,1024]{1,0:T(8,128)S(1)} %second.1.second_ref), channel_id=1, source_target_pairs={{0,1},{1,0},{2,3},{3,2},{4,5},{5,4},{6,7},{7,6},{8,9},{9,8},{10,11... | collective-permute-start | bytes 196616 | tf_op jit(solution)/shard_map/ppermute | solution.py:108
  21.4 0.0 collective-permute-done.1.first_other_ref
  21.4 0.0 slice-done
  21.4 0.0 slice-done.1
  21.4 0.0 slice-done.2
  21.4 1.0 %slice-done.3 = s8[4194304]{0:T(1024)(128)(4,1)S(1)} async-done(((s8[16777216]{0:T(1024)(128)(4,1)}), s8[4194304]{0:T(1024)(128)(4,1)S(1)}, s32[]{:S(2)}) %slice-start.3) | async-done | bytes 4194328
  22.4 1.2 %down.1.sum_ref = f32[16,4096]{1,0:T(8,128)S(1)} custom-call(f32[16,3072]{1,0:T(8,128)S(1)} %first.1.first_ref, f32[16,3072]{1,0:T(8,128)S(1)} %collective-permute-done.1.first_other_ref, bf16[2048,4096]{1,0:T(8,128)(2,1)S(1)} %bitcast.2), custom_call_target="tpu_custom_call" | custom-call | tf_op jit(solution)/shard_map/down/pallas_call | solution.py:14
  23.6 0.0 collective-permute-done.2.second_other_ref
  23.6 1.2 %add.1 = bf16[8,2,4096]{2,1,0:T(2,128)(2,1)S(1)} custom-call(f32[16,3072]{1,0:T(8,128)S(1)} %first.1.first_ref, f32[16,3072]{1,0:T(8,128)S(1)} %collective-permute-done.1.first_other_ref, f32[16,1024]{1,0:T(8,128)S(1)} %second.1.second_ref, f32[16,1024]{1,0:T(8,128)S(1)} %collective-permute-done.2.second_other_ref, bf16[2048,4096]{1,0:T(8,128)(2,1)S(1)} %bitcast.2, ...), custom_call_target="tpu_custom_call" | custom-call | tf_op jit(solution)/shard_map/add/pallas_call | solution.py:14
  24.8 9.8 %all_to_all.11.parts_ref = bf16[8,2,4096]{2,1,0:T(2,128)(2,1)S(1)} all-to-all(bf16[8,2,4096]{2,1,0:T(2,128)(2,1)S(1)} %add.1), channel_id=1, replica_groups=mesh['rep'=2,'hid'=8,'wid'=2] {'hid'}, dimensions={0} | all-to-all | bytes 262144 | tf_op jit(solution)/shard_map/all_to_all | solution.py:180
  34.7 0.0 copy-done.2
  34.7 0.6 %finish.1 = f32[2,4096]{1,0:T(2,128)} custom-call(f32[2,4096]{1,0:T(2,128)S(1)} %copy-done.2, bf16[8,2,4096]{2,1,0:T(2,128)(2,1)S(1)} %all_to_all.11.parts_ref), custom_call_target="tpu_custom_call" | custom-call | tf_op jit(solution)/shard_map/finish/pallas_call | solution.py:14
  (1 shorter events, 0.0 us)
Async XLA Ops:
  0.0 1.6 %collective-permute-start = (f32[2,4096]{1,0:T(2,128)}, f32[2,4096]{1,0:T(2,128)S(1)}, u32[]{:S(2)}, u32[]{:S(2)}) collective-permute-start(f32[2,4096]{1,0:T(2,128)} %states_ref.1), channel_id=1, source_target_pairs={{0,1},{1,0},{2,3},{3,2},{4,5},{5,4},{6,7},{7,6},{8,9},{9,8},{10,11... | collective-permute-start | bytes 98312 | tf_op jit(solution)/shard_map/ppermute | solution.py:108
  0.5 15.8 %copy-start = (bf16[4096,2048]{1,0:T(8,128)(2,1)S(1)}, bf16[4096,2048]{1,0:T(8,128)(2,1)}, u32[]{:S(2)}) copy-start(bf16[4096,2048]{1,0:T(8,128)(2,1)} %up_ref.3) | copy-start | bytes 50331652
  0.5 15.8 %copy-start.1 = (bf16[4096,2048]{1,0:T(8,128)(2,1)S(1)}, bf16[4096,2048]{1,0:T(8,128)(2,1)}, u32[]{:S(2)}) copy-start(bf16[4096,2048]{1,0:T(8,128)(2,1)} %gate_ref.1) | copy-start | bytes 50331652
  16.3 5.1 %slice-start = ((s8[16777216]{0:T(1024)(128)(4,1)}), s8[4194304]{0:T(1024)(128)(4,1)S(1)}, s32[]{:S(2)}) async-start(s8[16777216]{0:T(1024)(128)(4,1)} %bitcast.1), calls=%async_computation.2 | async-start | bytes 8388608
  16.3 5.1 %slice-start.1 = ((s8[16777216]{0:T(1024)(128)(4,1)}), s8[4194304]{0:T(1024)(128)(4,1)S(1)}, s32[]{:S(2)}) async-start(s8[16777216]{0:T(1024)(128)(4,1)} %bitcast.1), calls=%async_computation.3 | async-start | bytes 8388608
  16.3 5.1 %slice-start.2 = ((s8[16777216]{0:T(1024)(128)(4,1)}), s8[4194304]{0:T(1024)(128)(4,1)S(1)}, s32[]{:S(2)}) async-start(s8[16777216]{0:T(1024)(128)(4,1)} %bitcast.1), calls=%async_computation.4 | async-start | bytes 8388608
  19.7 2.7 %slice-start.3 = ((s8[16777216]{0:T(1024)(128)(4,1)}), s8[4194304]{0:T(1024)(128)(4,1)S(1)}, s32[]{:S(2)}) async-start(s8[16777216]{0:T(1024)(128)(4,1)} %bitcast.1), calls=%async_computation.5 | async-start | bytes 8388608
  19.7 1.7 %collective-permute-start.1 = (f32[16,3072]{1,0:T(8,128)S(1)}, f32[16,3072]{1,0:T(8,128)S(1)}, u32[]{:S(2)}, u32[]{:S(2)}) collective-permute-start(f32[16,3072]{1,0:T(8,128)S(1)} %first.1.first_ref), channel_id=1, source_target_pairs={{0,1},{1,0},{2,3},{3,2},{4,5},{5,4},{6,7},{7,6},{8,9},{9,8},{10,11... | collective-permute-start | bytes 589832 | tf_op jit(solution)/shard_map/ppermute | solution.py:108
  20.9 13.8 %copy-start.2 = (f32[2,4096]{1,0:T(2,128)S(1)}, f32[2,4096]{1,0:T(2,128)}, u32[]{:S(2)}) copy-start(f32[2,4096]{1,0:T(2,128)} %states_ref.1) | copy-start | bytes 98308
  20.9 2.7 %collective-permute-start.2 = (f32[16,1024]{1,0:T(8,128)S(1)}, f32[16,1024]{1,0:T(8,128)S(1)}, u32[]{:S(2)}, u32[]{:S(2)}) collective-permute-start(f32[16,1024]{1,0:T(8,128)S(1)} %second.1.second_ref), channel_id=1, source_target_pairs={{0,1},{1,0},{2,3},{3,2},{4,5},{5,4},{6,7},{7,6},{8,9},{9,8},{10,11... | collective-permute-start | bytes 196616 | tf_op jit(solution)/shard_map/ppermute | solution.py:108

commit v3 on v2

--- a/solution.py
+++ b/solution.py
@@ -1,3 +1,5 @@
+import functools
+
 import jax
 import jax.numpy as jnp
 from jax import lax
@@ -50,41 +52,26 @@
         out_ref[k] = normed
 
 
-def first_kernel(gathered_ref, gate_ref, up_ref, out_ref):
-    streams, total = out_ref.shape
-    width = gate_ref.shape[1]
+def project_kernel(gathered_ref, gate_ref, up_ref, *out_refs):
+    streams, double = out_refs[0].shape
+    count = double // 2
     x = gathered_ref[...].reshape(streams, gate_ref.shape[0])
-    out_ref[:, :width] = dot(x, gate_ref[...])
-    out_ref[:, width:] = dot(x, up_ref[:, : total - width])
+    for side, weight_ref in enumerate((gate_ref, up_ref)):
+        product = dot(x, weight_ref[...])
+        for k, out_ref in enumerate(out_refs):
+            out_ref[:, side * count : (side + 1) * count] = product[:, k * count : (k + 1) * count]
 
 
-def second_kernel(gathered_ref, up_ref, *refs):
+def down_kernel(start, mine_ref, other_ref, down_ref, *refs):
+    count = mine_ref.shape[1] // 2
+    total = mine_ref[...] + other_ref[...]
+    gate, up = total[:, :count], total[:, count:]
+    hidden = (gate / (1 + jnp.exp(-gate)) * up).astype(BF16)
+    product = dot(hidden, down_ref[start : start + count, :])
+    if len(refs) == 2:
+        product += refs[0][...]
     out_ref = refs[-1]
-    streams, count = out_ref.shape
-    x = gathered_ref[...].reshape(streams, up_ref.shape[0])
-    out_ref[...] = dot(x, up_ref[:, up_ref.shape[1] - count :])
-
-
-def activate(gate, up):
-    return (gate / (1 + jnp.exp(-gate)) * up).astype(BF16)
-
-
-def down_kernel(first_ref, first_other_ref, down_ref, out_ref):
-    width = down_ref.shape[0]
-    count = first_ref.shape[1] - width
-    gate = first_ref[:, :count] + first_other_ref[:, :count]
-    up = first_ref[:, width:] + first_other_ref[:, width:]
-    out = dot(activate(gate, up), down_ref[:count, :])
-    out_ref[...] = out.astype(out_ref.dtype).reshape(out_ref.shape)
-
-
-def add_kernel(first_ref, first_other_ref, second_ref, second_other_ref, down_ref, sum_ref, out_ref):
-    width = down_ref.shape[0]
-    count = first_ref.shape[1] - width
-    gate = first_ref[:, count:width] + first_other_ref[:, count:width]
-    up = second_ref[...] + second_other_ref[...]
-    out = sum_ref[...] + dot(activate(gate, up), down_ref[count:, :])
-    out_ref[...] = out.astype(out_ref.dtype).reshape(out_ref.shape)
+    out_ref[...] = product.astype(out_ref.dtype).reshape(out_ref.shape)
 
 
 def finish_kernel(states_ref, parts_ref, out_ref):
@@ -133,51 +120,34 @@
         )
         gathered = lax.all_to_all(normed, "hid", 0, 0)
 
-        first = call(
-            first_kernel,
-            struct((streams, width + count), F32),
+        pieces = width // count
+        part = struct((streams, 2 * count), F32)
+        parts = call(
+            project_kernel,
+            (part,) * pieces,
             gathered,
             gate_weight,
             up_weight,
-            name="first",
+            name="project",
             limit=17 << 18,
         )
-        first_other = swap(first)
-        out = struct((hid, rows, half), BF16)
-        if count == width:
-            mixed = call(down_kernel, out, first, first_other, down_weight, name="down")
-        else:
-            second = call(
-                second_kernel,
-                struct((streams, width - count), F32),
-                gathered,
-                up_weight,
-                name="second",
-                limit=4 << 20,
+        others = [swap(value) for value in parts]
+        mixed = ()
+        for k in range(pieces):
+            last = k == pieces - 1
+            mixed = (
+                call(
+                    functools.partial(down_kernel, k * count),
+                    struct((hid, rows, half), BF16) if last else struct((streams, half), F32),
+                    parts[k],
+                    others[k],
+                    down_weight,
+                    *mixed,
+                    name=f"down{k}",
+                    limit=3 << 20,
+                ),
             )
-            second_other = swap(second)
-            mixed = call(
-                down_kernel,
-                struct((streams, half), F32),
-                first,
-                first_other,
-                down_weight,
-                name="down",
-                limit=3 << 20,
-            )
-            mixed = call(
-                add_kernel,
-                out,
-                first,
-                first_other,
-                second,
-                second_other,
-                down_weight,
-                mixed,
-                name="add",
-                limit=3 << 20,
-            )
-        summands = lax.all_to_all(mixed, "hid", 0, 0)
+        summands = lax.all_to_all(*mixed, "hid", 0, 0)
         return call(finish_kernel, struct((rows, half), F32), states, summands, name="finish")
 
     return jax.shard_map(

time: 35.6 us -> 35.4 us (level)
  local copies, waits for them, and re-layouts: 0.99 us -> 0.01 us
  waiting for transfers between devices: 0.02 us -> 0.85 us
    unnamed x14 -> x8, local copies, waits for them, and re-layouts: 0.99 us -> 0.01 us
    ppermute x3, waiting for transfers between devices: 0.02 us -> 0.85 us  [swap(): return lax.ppermute(value, 'wid', [(0, 1), (1, 0)])]
    pallas_call x7 -> x6, Pallas kernels: 8.85 us -> 8.73 us  [call(): pl.pallas_call(kernel, out_shape=out, in_specs=[pl.BlockSpec(memory_space...]
  transfers between devices with their start and end apart: 3 -> 3, of which waited for: 0 -> 1; matrix products, arithmetic and copies ran while one was open for 0% -> 0% of each run, Pallas kernels for 10% -> 6%
where the time goes in v3:
time: 35.4 us; the launch traced here: 35.2 us
  blocking collectives  24.5 us (69%)
  Pallas kernels  8.73 us (25%)
  starting transfers between devices  1.02 us (3%)
  waiting for transfers between devices  0.85 us (2%)
    all_to_all x1, blocking collectives, local(): gathered = lax.all_to_all(normed, 'hid', 0, 0)  14.5 us
    all_to_all x1, blocking collectives, local(): summands = lax.all_to_all(*mixed, 'hid', 0, 0)  9.97 us
    pallas_call x6, Pallas kernels, call(): pl.pallas_call(kernel, out_shape=out, in_specs=[pl.BlockSpec(memory_space...  8.73 us
    ppermute x3, starting transfers between devices, swap(): return lax.ppermute(value, 'wid', [(0, 1), (1, 0)])  1.02 us
    ppermute x3, waiting for transfers between devices, swap(): return lax.ppermute(value, 'wid', [(0, 1), (1, 0)])  0.85 us
  transfers between devices with their start and end apart: 3, of which 1 were waited for; matrix products, arithmetic and copies ran while one was open for 0% of the time, Pallas kernels for 6%

profile of v3, /device:TPU:0, one launch (start us, length us, event | category | flops | bytes accessed | tf_op | source)
XLA Modules:
  0.0 35.2 jit_solution(2844187294277965517)
XLA Ops:
  0.0 0.5 %collective-permute-start = (f32[2,4096]{1,0:T(2,128)}, f32[2,4096]{1,0:T(2,128)S(1)}, u32[]{:S(2)}, u32[]{:S(2)}) collective-permute-start(f32[2,4096]{1,0:T(2,128)} %states_ref.1), channel_id=1, source_target_pairs={{0,1},{1,0},{2,3},{3,2},{4,5},{5,4},{6,7},{7,6},{8,9},{9,8},{10,11... | collective-permute-start | bytes 98312 | tf_op jit(solution)/shard_map/ppermute | solution.py:95
  0.5 0.0 copy-start.1
  0.5 0.0 copy-start.2
  0.5 1.0 %load.1 = (f32[2,4096]{1,0:T(2,128)S(1)}, f32[2,1]{1,0:T(2,128)S(1)}) custom-call(f32[2,4096]{1,0:T(2,128)} %states_ref.1, f32[1,4096]{1,0:T(1,128)} %bitcast.1), custom_call_target="tpu_custom_call" | custom-call | flops 99999997952 | tf_op jit(solution)/shard_map/load/pallas_call | solution.py:16
  1.5 0.0 collective-permute-done.others_ref
  1.6 0.2 prepare.1
  1.8 14.5 %all_to_all.10.gathered_ref = bf16[8,2,4096]{2,1,0:T(2,128)(2,1)S(1)} all-to-all(bf16[8,2,4096]{2,1,0:T(2,128)(2,1)S(1)} %prepare.1), channel_id=1, replica_groups=mesh['rep'=2,'hid'=8,'wid'=2] {'hid'}, dimensions={0} | all-to-all | bytes 262144 | tf_op jit(solution)/shard_map/all_to_all | solution.py:121
  16.3 0.0 copy-done.1
  16.3 0.0 copy-done.2
  16.3 0.0 copy-start
  16.3 4.4 %project.1 = (f32[16,2048]{1,0:T(8,128)S(1)}, f32[16,2048]{1,0:T(8,128)S(1)}) custom-call(bf16[8,2,4096]{2,1,0:T(2,128)(2,1)S(1)} %all_to_all.10.gathered_ref, bf16[4096,2048]{1,0:T(8,128)(2,1)S(1)} %copy-done.1, bf16[4096,2048]{1,0:T(8,128)(2,1)S(1)} %copy-done.2), custom_call_target="tpu_custom_call" | custom-call | tf_op jit(solution)/shard_map/project/pallas_call | solution.py:16
  20.8 0.0 collective-permute-start.2
  20.8 0.0 copy-start.3
  20.8 0.5 %collective-permute-start.1 = (f32[16,2048]{1,0:T(8,128)S(1)}, f32[16,2048]{1,0:T(8,128)S(1)}, u32[]{:S(2)}, u32[]{:S(2)}) collective-permute-start(f32[16,2048]{1,0:T(8,128)S(1)} %get-tuple-element.11.mine_ref), channel_id=1, source_target_pairs={{0,1},{1,0},{2,3},{3,2},{4,5},{5,4},{6,7},{7,6},{8,9},{9,8},{10,11... | collective-permute-start | bytes 393224 | tf_op jit(solution)/shard_map/ppermute | solution.py:95
  21.3 0.8 %collective-permute-done.2.other_ref = f32[16,2048]{1,0:T(8,128)S(1)} collective-permute-done((f32[16,2048]{1,0:T(8,128)S(1)}, f32[16,2048]{1,0:T(8,128)S(1)}, u32[]{:S(2)}, u32[]{:S(2)}) %collective-permute-start.2) | collective-permute-done | bytes 131104 | tf_op jit(solution)/shard_map/ppermute | solution.py:95
  22.1 0.0 copy-done
  22.1 1.2 %down0.1.refs_0_ = f32[16,4096]{1,0:T(8,128)S(1)} custom-call(f32[16,2048]{1,0:T(8,128)S(1)} %get-tuple-element.12.mine_ref, f32[16,2048]{1,0:T(8,128)S(1)} %collective-permute-done.2.other_ref, bf16[2048,4096]{1,0:T(8,128)(2,1)S(1)} %copy-done), custom_call_target="tpu_custom_call" | custom-call | tf_op jit(solution)/shard_map/down0/pallas_call | solution.py:16
  23.3 0.0 collective-permute-done.1.other_ref
  23.3 1.2 %down1.1 = bf16[8,2,4096]{2,1,0:T(2,128)(2,1)S(1)} custom-call(f32[16,2048]{1,0:T(8,128)S(1)} %get-tuple-element.11.mine_ref, f32[16,2048]{1,0:T(8,128)S(1)} %collective-permute-done.1.other_ref, bf16[2048,4096]{1,0:T(8,128)(2,1)S(1)} %copy-done, f32[16,4096]{1,0:T(8,128)S(1)} %down0.1.refs_0_), custom_call_target="tpu_custom_call" | custom-call | tf_op jit(solution)/shard_map/down1/pallas_call | solution.py:16
  24.5 10.0 %all_to_all.11.parts_ref = bf16[8,2,4096]{2,1,0:T(2,128)(2,1)S(1)} all-to-all(bf16[8,2,4096]{2,1,0:T(2,128)(2,1)S(1)} %down1.1), channel_id=1, replica_groups=mesh['rep'=2,'hid'=8,'wid'=2] {'hid'}, dimensions={0} | all-to-all | bytes 262144 | tf_op jit(solution)/shard_map/all_to_all | solution.py:150
  34.5 0.0 copy-done.3
  34.5 0.6 %finish.1 = f32[2,4096]{1,0:T(2,128)} custom-call(f32[2,4096]{1,0:T(2,128)S(1)} %copy-done.3, bf16[8,2,4096]{2,1,0:T(2,128)(2,1)S(1)} %all_to_all.11.parts_ref), custom_call_target="tpu_custom_call" | custom-call | tf_op jit(solution)/shard_map/finish/pallas_call | solution.py:16
Async XLA Ops:
  0.0 1.6 %collective-permute-start = (f32[2,4096]{1,0:T(2,128)}, f32[2,4096]{1,0:T(2,128)S(1)}, u32[]{:S(2)}, u32[]{:S(2)}) collective-permute-start(f32[2,4096]{1,0:T(2,128)} %states_ref.1), channel_id=1, source_target_pairs={{0,1},{1,0},{2,3},{3,2},{4,5},{5,4},{6,7},{7,6},{8,9},{9,8},{10,11... | collective-permute-start | bytes 98312 | tf_op jit(solution)/shard_map/ppermute | solution.py:95
  0.5 15.8 %copy-start.1 = (bf16[4096,2048]{1,0:T(8,128)(2,1)S(1)}, bf16[4096,2048]{1,0:T(8,128)(2,1)}, u32[]{:S(2)}) copy-start(bf16[4096,2048]{1,0:T(8,128)(2,1)} %gate_ref.1) | copy-start | bytes 50331652
  0.5 15.8 %copy-start.2 = (bf16[4096,2048]{1,0:T(8,128)(2,1)S(1)}, bf16[4096,2048]{1,0:T(8,128)(2,1)}, u32[]{:S(2)}) copy-start(bf16[4096,2048]{1,0:T(8,128)(2,1)} %up_ref.1) | copy-start | bytes 50331652
  16.3 5.8 %copy-start = (bf16[2048,4096]{1,0:T(8,128)(2,1)S(1)}, bf16[2048,4096]{1,0:T(8,128)(2,1)}, u32[]{:S(2)}) copy-start(bf16[2048,4096]{1,0:T(8,128)(2,1)} %down_ref.3) | copy-start | bytes 50331652
  20.8 1.4 %collective-permute-start.2 = (f32[16,2048]{1,0:T(8,128)S(1)}, f32[16,2048]{1,0:T(8,128)S(1)}, u32[]{:S(2)}, u32[]{:S(2)}) collective-permute-start(f32[16,2048]{1,0:T(8,128)S(1)} %get-tuple-element.12.mine_ref), channel_id=1, source_target_pairs={{0,1},{1,0},{2,3},{3,2},{4,5},{5,4},{6,7},{7,6},{8,9},{9,8},{10,11... | collective-permute-start | bytes 393224 | tf_op jit(solution)/shard_map/ppermute | solution.py:95
  20.8 13.8 %copy-start.3 = (f32[2,4096]{1,0:T(2,128)S(1)}, f32[2,4096]{1,0:T(2,128)}, u32[]{:S(2)}) copy-start(f32[2,4096]{1,0:T(2,128)} %states_ref.1) | copy-start | bytes 98308
  20.8 2.6 %collective-permute-start.1 = (f32[16,2048]{1,0:T(8,128)S(1)}, f32[16,2048]{1,0:T(8,128)S(1)}, u32[]{:S(2)}, u32[]{:S(2)}) collective-permute-start(f32[16,2048]{1,0:T(8,128)S(1)} %get-tuple-element.11.mine_ref), channel_id=1, source_target_pairs={{0,1},{1,0},{2,3},{3,2},{4,5},{5,4},{6,7},{7,6},{8,9},{9,8},{10,11... | collective-permute-start | bytes 393224 | tf_op jit(solution)/shard_map/ppermute | solution.py:95

commit v4 on v3

--- a/solution.py
+++ b/solution.py
@@ -53,13 +53,14 @@
 
 
 def project_kernel(gathered_ref, gate_ref, up_ref, *out_refs):
-    streams, double = out_refs[0].shape
-    count = double // 2
-    x = gathered_ref[...].reshape(streams, gate_ref.shape[0])
+    x = gathered_ref[...].reshape(out_refs[0].shape[0], gate_ref.shape[0])
     for side, weight_ref in enumerate((gate_ref, up_ref)):
         product = dot(x, weight_ref[...])
-        for k, out_ref in enumerate(out_refs):
-            out_ref[:, side * count : (side + 1) * count] = product[:, k * count : (k + 1) * count]
+        start = 0
+        for out_ref in out_refs:
+            count = out_ref.shape[1] // 2
+            out_ref[:, side * count : (side + 1) * count] = product[:, start : start + count]
+            start += count
 
 
 def down_kernel(start, mine_ref, other_ref, down_ref, *refs):
@@ -88,7 +89,7 @@
         rows, half = states.shape
         width = gate_weight.shape[1]
         streams = rows * hid
-        count = width // 2 if width % 256 == 0 else width
+        counts = (width // 4, width - width // 4) if width % 512 == 0 else (width,)
         struct = jax.ShapeDtypeStruct
 
         def swap(value):
@@ -120,11 +121,10 @@
         )
         gathered = lax.all_to_all(normed, "hid", 0, 0)
 
-        pieces = width // count
-        part = struct((streams, 2 * count), F32)
+        pieces = len(counts)
         parts = call(
             project_kernel,
-            (part,) * pieces,
+            tuple(struct((streams, 2 * count), F32) for count in counts),
             gathered,
             gate_weight,
             up_weight,
@@ -137,7 +137,7 @@
             last = k == pieces - 1
             mixed = (
                 call(
-                    functools.partial(down_kernel, k * count),
+                    functools.partial(down_kernel, sum(counts[:k])),
                     struct((hid, rows, half), BF16) if last else struct((streams, half), F32),
                     parts[k],
                     others[k],

time: 35.4 us -> 35.7 us (level)
  transfers between devices with their start and end apart: 3 -> 3, of which waited for: 1 -> 1; matrix products, arithmetic and copies ran while one was open for 0% -> 0% of each run, Pallas kernels for 6% -> 5%
where the time goes in v4:
time: 35.7 us; the launch traced here: 35.4 us
  blocking collectives  24.6 us (69%)
  Pallas kernels  8.73 us (24%)
  waiting for transfers between devices  1.04 us (3%)
  starting transfers between devices  1.02 us (3%)
    all_to_all x1, blocking collectives, local(): gathered = lax.all_to_all(normed, 'hid', 0, 0)  14.5 us
    all_to_all x1, blocking collectives, local(): summands = lax.all_to_all(*mixed, 'hid', 0, 0)  10.1 us
    pallas_call x6, Pallas kernels, call(): pl.pallas_call(kernel, out_shape=out, in_specs=[pl.BlockSpec(memory_space...  8.73 us
    ppermute x3, waiting for transfers between devices, swap(): return lax.ppermute(value, 'wid', [(0, 1), (1, 0)])  1.04 us
    ppermute x3, starting transfers between devices, swap(): return lax.ppermute(value, 'wid', [(0, 1), (1, 0)])  1.02 us
  transfers between devices with their start and end apart: 3, of which 1 were waited for; matrix products, arithmetic and copies ran while one was open for 0% of the time, Pallas kernels for 5%

profile of v4, /device:TPU:0, one launch (start us, length us, event | category | flops | bytes accessed | tf_op | source)
XLA Modules:
  0.0 35.4 jit_solution(2695064039288533942)
XLA Ops:
  0.0 0.5 %collective-permute-start = (f32[2,4096]{1,0:T(2,128)}, f32[2,4096]{1,0:T(2,128)S(1)}, u32[]{:S(2)}, u32[]{:S(2)}) collective-permute-start(f32[2,4096]{1,0:T(2,128)} %states_ref.1), channel_id=1, source_target_pairs={{0,1},{1,0},{2,3},{3,2},{4,5},{5,4},{6,7},{7,6},{8,9},{9,8},{10,11... | collective-permute-start | bytes 98312 | tf_op jit(solution)/shard_map/ppermute | solution.py:96
  0.5 0.0 copy-start.1
  0.5 0.0 copy-start.2
  0.5 1.0 %load.1 = (f32[2,4096]{1,0:T(2,128)S(1)}, f32[2,1]{1,0:T(2,128)S(1)}) custom-call(f32[2,4096]{1,0:T(2,128)} %states_ref.1, f32[1,4096]{1,0:T(1,128)} %bitcast.1), custom_call_target="tpu_custom_call" | custom-call | flops 99999997952 | tf_op jit(solution)/shard_map/load/pallas_call | solution.py:16
  1.5 0.0 collective-permute-done.others_ref
  1.6 0.2 prepare.1
  1.8 14.5 %all_to_all.10.gathered_ref = bf16[8,2,4096]{2,1,0:T(2,128)(2,1)S(1)} all-to-all(bf16[8,2,4096]{2,1,0:T(2,128)(2,1)S(1)} %prepare.1), channel_id=1, replica_groups=mesh['rep'=2,'hid'=8,'wid'=2] {'hid'}, dimensions={0} | all-to-all | bytes 262144 | tf_op jit(solution)/shard_map/all_to_all | solution.py:122
  16.3 0.0 copy-done.1
  16.3 0.0 copy-done.2
  16.3 0.0 copy-start
  16.3 4.4 %project.1 = (f32[16,1024]{1,0:T(8,128)S(1)}, f32[16,3072]{1,0:T(8,128)S(1)}) custom-call(bf16[8,2,4096]{2,1,0:T(2,128)(2,1)S(1)} %all_to_all.10.gathered_ref, bf16[4096,2048]{1,0:T(8,128)(2,1)S(1)} %copy-done.1, bf16[4096,2048]{1,0:T(8,128)(2,1)S(1)} %copy-done.2), custom_call_target="tpu_custom_call" | custom-call | tf_op jit(solution)/shard_map/project/pallas_call | solution.py:16
  20.8 0.0 collective-permute-start.1
  20.8 0.0 copy-start.3
  20.8 0.5 %collective-permute-start.2 = (f32[16,1024]{1,0:T(8,128)S(1)}, f32[16,1024]{1,0:T(8,128)S(1)}, u32[]{:S(2)}, u32[]{:S(2)}) collective-permute-start(f32[16,1024]{1,0:T(8,128)S(1)} %get-tuple-element.12.mine_ref), channel_id=1, source_target_pairs={{0,1},{1,0},{2,3},{3,2},{4,5},{5,4},{6,7},{7,6},{8,9},{9,8},{10,11... | collective-permute-start | bytes 196616 | tf_op jit(solution)/shard_map/ppermute | solution.py:96
  21.3 1.0 %collective-permute-done.2.other_ref = f32[16,1024]{1,0:T(8,128)S(1)} collective-permute-done((f32[16,1024]{1,0:T(8,128)S(1)}, f32[16,1024]{1,0:T(8,128)S(1)}, u32[]{:S(2)}, u32[]{:S(2)}) %collective-permute-start.2) | collective-permute-done | bytes 65568 | tf_op jit(solution)/shard_map/ppermute | solution.py:96
  22.3 0.0 copy-done
  22.3 0.6 %down0.1.refs_0_ = f32[16,4096]{1,0:T(8,128)S(1)} custom-call(f32[16,1024]{1,0:T(8,128)S(1)} %get-tuple-element.12.mine_ref, f32[16,1024]{1,0:T(8,128)S(1)} %collective-permute-done.2.other_ref, bf16[2048,4096]{1,0:T(8,128)(2,1)S(1)} %copy-done), custom_call_target="tpu_custom_call" | custom-call | tf_op jit(solution)/shard_map/down0/pallas_call | solution.py:16
  23.0 0.0 collective-permute-done.1.other_ref
  23.0 1.8 %down1.1 = bf16[8,2,4096]{2,1,0:T(2,128)(2,1)S(1)} custom-call(f32[16,3072]{1,0:T(8,128)S(1)} %get-tuple-element.11.mine_ref, f32[16,3072]{1,0:T(8,128)S(1)} %collective-permute-done.1.other_ref, bf16[2048,4096]{1,0:T(8,128)(2,1)S(1)} %copy-done, f32[16,4096]{1,0:T(8,128)S(1)} %down0.1.refs_0_), custom_call_target="tpu_custom_call" | custom-call | tf_op jit(solution)/shard_map/down1/pallas_call | solution.py:16
  24.7 10.1 %all_to_all.11.parts_ref = bf16[8,2,4096]{2,1,0:T(2,128)(2,1)S(1)} all-to-all(bf16[8,2,4096]{2,1,0:T(2,128)(2,1)S(1)} %down1.1), channel_id=1, replica_groups=mesh['rep'=2,'hid'=8,'wid'=2] {'hid'}, dimensions={0} | all-to-all | bytes 262144 | tf_op jit(solution)/shard_map/all_to_all | solution.py:150
  34.8 0.0 copy-done.3
  34.8 0.6 %finish.1 = f32[2,4096]{1,0:T(2,128)} custom-call(f32[2,4096]{1,0:T(2,128)S(1)} %copy-done.3, bf16[8,2,4096]{2,1,0:T(2,128)(2,1)S(1)} %all_to_all.11.parts_ref), custom_call_target="tpu_custom_call" | custom-call | tf_op jit(solution)/shard_map/finish/pallas_call | solution.py:16
Async XLA Ops:
  0.0 1.6 %collective-permute-start = (f32[2,4096]{1,0:T(2,128)}, f32[2,4096]{1,0:T(2,128)S(1)}, u32[]{:S(2)}, u32[]{:S(2)}) collective-permute-start(f32[2,4096]{1,0:T(2,128)} %states_ref.1), channel_id=1, source_target_pairs={{0,1},{1,0},{2,3},{3,2},{4,5},{5,4},{6,7},{7,6},{8,9},{9,8},{10,11... | collective-permute-start | bytes 98312 | tf_op jit(solution)/shard_map/ppermute | solution.py:96
  0.5 15.8 %copy-start.1 = (bf16[4096,2048]{1,0:T(8,128)(2,1)S(1)}, bf16[4096,2048]{1,0:T(8,128)(2,1)}, u32[]{:S(2)}) copy-start(bf16[4096,2048]{1,0:T(8,128)(2,1)} %gate_ref.1) | copy-start | bytes 50331652
  0.5 15.8 %copy-start.2 = (bf16[4096,2048]{1,0:T(8,128)(2,1)S(1)}, bf16[4096,2048]{1,0:T(8,128)(2,1)}, u32[]{:S(2)}) copy-start(bf16[4096,2048]{1,0:T(8,128)(2,1)} %up_ref.1) | copy-start | bytes 50331652
  16.3 6.0 %copy-start = (bf16[2048,4096]{1,0:T(8,128)(2,1)S(1)}, bf16[2048,4096]{1,0:T(8,128)(2,1)}, u32[]{:S(2)}) copy-start(bf16[2048,4096]{1,0:T(8,128)(2,1)} %down_ref.3) | copy-start | bytes 50331652
  20.8 2.2 %collective-permute-start.1 = (f32[16,3072]{1,0:T(8,128)S(1)}, f32[16,3072]{1,0:T(8,128)S(1)}, u32[]{:S(2)}, u32[]{:S(2)}) collective-permute-start(f32[16,3072]{1,0:T(8,128)S(1)} %get-tuple-element.11.mine_ref), channel_id=1, source_target_pairs={{0,1},{1,0},{2,3},{3,2},{4,5},{5,4},{6,7},{7,6},{8,9},{9,8},{10,11... | collective-permute-start | bytes 589832 | tf_op jit(solution)/shard_map/ppermute | solution.py:96
  20.8 14.0 %copy-start.3 = (f32[2,4096]{1,0:T(2,128)S(1)}, f32[2,4096]{1,0:T(2,128)}, u32[]{:S(2)}) copy-start(f32[2,4096]{1,0:T(2,128)} %states_ref.1) | copy-start | bytes 98308
  20.8 1.5 %collective-permute-start.2 = (f32[16,1024]{1,0:T(8,128)S(1)}, f32[16,1024]{1,0:T(8,128)S(1)}, u32[]{:S(2)}, u32[]{:S(2)}) collective-permute-start(f32[16,1024]{1,0:T(8,128)S(1)} %get-tuple-element.12.mine_ref), channel_id=1, source_target_pairs={{0,1},{1,0},{2,3},{3,2},{4,5},{5,4},{6,7},{7,6},{8,9},{9,8},{10,11... | collective-permute-start | bytes 196616 | tf_op jit(solution)/shard_map/ppermute | solution.py:96
